TPU v7x, 32 devices: a whole 2x2x4 slice. The times are simulated.
32 devices in a mesh: row: 8 (over z, y), col: 4 (over x, core).
Axes of the slice: x: 2, y: 2, z: 4, core: 2. Of those that a mesh axis runs over, the one named last changes fastest.
Arguments:
- start_block: float32 [64, 16, 128], P(('row', 'col')), may hold values from -6 to 6
- blocks: float32 [8, 4, 58, 128, 128], P('row', 'col'), as said below
- slot_row: int32 [8, 4, 58], P('row', 'col'), may hold values from 0 to 7, as said below
- slot_col: int32 [8, 4, 58], P('row', 'col'), may hold values from 0 to 15, as said below
- counts: int32 [8, 4], P('row', 'col'), may hold values from 34 to 58, as said below
Outputs:
- alphas: float32 [2, 16, 16], replicated
- betas: float32 [2, 16, 16], replicated
- next_block: float32 [64, 16, 128], P(('row', 'col'))
Inputs may be any that keep to these rules, and one draw needn't show every extreme that they name: `blocks`: over all cells the live slots list each nonzero block of a symmetric matrix exactly once: block (J, I) is listed exactly when (I, J) is, holding its transpose. Slots at or past a cell's count hold finite values that are no part of H. `counts`: live slots of a cell come first; in every draw some cell has all 58 slots live. `slot_row`: for live slots, the block row within the cell's row group of 8 block rows. `slot_col`: for live slots, the position within the cell's column group of 16 block columns, as in the first step.
All inputs are finite; a program needn't handle non-finite values.
Results may differ from a plain program's by a relative error of at most 0.0003.
Values sent between devices are 32-bit elements; how exact they have to be, the bound alone decides.
A program may use at most 64 MiB of HBM per device.

v0:
```python
import jax
import jax.numpy as jnp
from jax import lax
from jax.sharding import PartitionSpec as P

ITERS = 2
highest = lax.Precision.HIGHEST


def matmul(left, right):
    return jnp.dot(left, right, precision=highest, preferred_element_type=jnp.float32)


def local_gram(left, right):
    return jnp.einsum(
        "bki,bli->kl", left, right, precision=highest, preferred_element_type=jnp.float32
    )


def on_device(start_block, blocks, slot_row, slot_col, counts):
    matrix_tiles = blocks[0, 0]
    rows_local = slot_row[0, 0]
    cols_local = slot_col[0, 0]
    capacity = matrix_tiles.shape[0]
    active = lax.iota(jnp.int32, capacity) < counts[0, 0]
    piece_rows = start_block.shape[0]
    vec_count = start_block.shape[1]
    orbitals = start_block.shape[2]
    row_total = float(piece_rows * lax.axis_size("row") * lax.axis_size("col") * orbitals)
    identity = jnp.eye(vec_count, dtype=jnp.float32)
    start_mean = lax.psum(local_gram(start_block, start_block), ("row", "col")) / row_total
    factor = jnp.linalg.cholesky(start_mean)
    inverse = jax.scipy.linalg.solve_triangular(factor, identity, lower=True)
    vectors = jnp.einsum(
        "kl,bli->bki", inverse, start_block, precision=highest, preferred_element_type=jnp.float32
    )
    previous = jnp.zeros(vectors.shape, jnp.float32)
    beta_prev = jnp.zeros((vec_count, vec_count), jnp.float32)
    alpha_list = []
    beta_list = []
    for iteration in range(ITERS):
        gathered = lax.all_gather(vectors, "row", axis=0, tiled=True)
        operate_product = jnp.einsum(
            "sij,skj->ski",
            matrix_tiles,
            gathered[cols_local],
            precision=highest,
            preferred_element_type=jnp.float32,
        )
        targets = lax.iota(jnp.int32, lax.axis_size("col") * piece_rows)
        selector = ((rows_local[None, :] == targets[:, None]) & active[None, :]).astype(jnp.float32)
        image_block = lax.psum_scatter(
            jnp.einsum(
                "rs,ski->rki",
                selector,
                operate_product,
                precision=highest,
                preferred_element_type=jnp.float32,
            ),
            "col",
            scatter_dimension=0,
            tiled=True,
        )
        stacked = jnp.concatenate([image_block, vectors, previous], axis=1)
        all_means = lax.psum(local_gram(stacked, stacked), ("row", "col")) / row_total
        yy_mean = all_means[:vec_count, :vec_count]
        vy_mean = all_means[vec_count : 2 * vec_count, :vec_count]
        py_mean = all_means[2 * vec_count :, :vec_count]
        vv_mean = all_means[vec_count : 2 * vec_count, vec_count : 2 * vec_count]
        pv_mean = all_means[2 * vec_count :, vec_count : 2 * vec_count]
        pp_mean = all_means[2 * vec_count :, 2 * vec_count :]
        residual = image_block - jnp.einsum(
            "lk,bli->bki", vy_mean, vectors, precision=highest, preferred_element_type=jnp.float32
        )
        residual = residual - jnp.einsum(
            "kl,bli->bki",
            beta_prev,
            previous,
            precision=highest,
            preferred_element_type=jnp.float32,
        )
        gram_mean = yy_mean - matmul(vy_mean.T, vy_mean) - matmul(vy_mean.T, vy_mean)
        gram_mean = gram_mean + matmul(matmul(vy_mean.T, vv_mean), vy_mean)
        gram_mean = gram_mean - matmul(py_mean.T, beta_prev.T) - matmul(beta_prev, py_mean)
        gram_mean = gram_mean + matmul(matmul(vy_mean.T, pv_mean.T), beta_prev.T)
        gram_mean = gram_mean + matmul(matmul(beta_prev, pv_mean), vy_mean)
        gram_mean = gram_mean + matmul(matmul(beta_prev, pp_mean), beta_prev.T)
        factor = jnp.linalg.cholesky(gram_mean)
        beta_block = factor.T
        inverse = jax.scipy.linalg.solve_triangular(factor, identity, lower=True)
        previous = vectors
        vectors = jnp.einsum(
            "kl,bli->bki", inverse, residual, precision=highest, preferred_element_type=jnp.float32
        )
        beta_prev = beta_block
        alpha_list.append(vy_mean)
        beta_list.append(beta_block)
    return (jnp.stack(alpha_list), jnp.stack(beta_list), vectors)


def solution(mesh):
    placed = (
        P(("row", "col"), None, None),
        P("row", "col", None, None, None),
        P("row", "col", None),
        P("row", "col", None),
        P("row", "col"),
    )
    return jax.shard_map(
        on_device,
        mesh=mesh,
        in_specs=placed,
        out_specs=(P(), P(), P(("row", "col"), None, None)),
        check_vma=False,
    )
```

profile of v0, /device:TPU:0, one launch (start us, length us, event | category | flops | bytes accessed | tf_op | source)
XLA Modules:
  0.0 285.7 jit_solution(17474431526224107313)
XLA Ops:
  8.7 42.0 %psum.21 = f32[16,16]{0,1:T(8,128)S(1)} all-reduce(f32[16,16]{0,1:T(8,128)S(1)} %convolution_bitcast_fusion.12), channel_id=1, replica_groups=mesh['row'=8,'col'=4] {'row','col'}, use_global_device_ids=true, to_apply=%region_0.0 | all-reduce | flops 256 | bytes 2048 | tf_op jit(solution)/shard_map/psum | solution.py:31
  50.8 1.5 cholesky.59
  53.6 1.2 custom-call.7
  55.1 30.6 %all_gather.6 = f32[16,16,128]{2,1,0:T(8,128)S(1)} all-gather(f32[2,16,128]{2,1,0:T(8,128)S(1)} %convolution_bitcast_fusion.8), channel_id=1, replica_groups=mesh['row'=8,'col'=4] {'row'}, dimensions={0}, use_global_device_ids=true | all-gather | bytes 147456 | tf_op jit(solution)/shard_map/all_gather | solution.py:42
  86.4 8.1 %fusion.2 = f32[58,16,128]{2,1,0:T(8,128)S(1)} fusion(f32[58,16,128]{2,1,0:T(8,128)S(1)} %gather_fusion, f32[1,1,58,128,128]{4,3,2,1,0:T(8,128)} %param.9), kind=kOutput, calls=%fused_computation.4 | convolution fusion | flops 182452224 | bytes 4751360 | tf_op jit(solution)/shard_map/sij,skj->ski/dot_general | solution.py:43
  95.6 19.3 %reduce-scatter.3.cloned.1.call-done = f32[2,16,128]{2,1,0:T(8,128)} async-done(((f32[8,16,128]{2,1,0:T(8,128)}), f32[2,16,128]{2,1,0:T(8,128)}) %reduce-scatter.3.cloned.1.call-update) | async-done | bytes 16400 | tf_op jit(solution)/shard_map/reduce_scatter | solution.py:52
  114.9 1.0 convolution_bitcast_fusion.1
  115.9 39.5 %psum.22 = f32[48,48]{0,1:T(8,128)S(1)} all-reduce(f32[48,48]{0,1:T(8,128)S(1)} %convolution_bitcast_fusion.1), channel_id=1, replica_groups=mesh['row'=8,'col'=4] {'row','col'}, use_global_device_ids=true, to_apply=%region_4.0 | all-reduce | flops 2304 | bytes 18432 | tf_op jit(solution)/shard_map/psum | solution.py:65
  156.4 0.9 fusion.7
  158.7 1.5 cholesky.70
  161.5 1.2 custom-call.8
  163.0 30.7 %all_gather.7 = f32[16,16,128]{2,1,0:T(8,128)S(1)} all-gather(f32[2,16,128]{2,1,0:T(8,128)S(1)} %convolution_bitcast_fusion.5), channel_id=1, replica_groups=mesh['row'=8,'col'=4] {'row'}, dimensions={0}, use_global_device_ids=true | all-gather | bytes 147456 | tf_op jit(solution)/shard_map/all_gather | solution.py:42
  194.4 8.1 %fusion = f32[58,16,128]{2,1,0:T(8,128)S(1)} fusion(f32[58,16,128]{2,1,0:T(8,128)S(1)} %gather_fusion.1, f32[1,1,58,128,128]{4,3,2,1,0:T(8,128)} %param.9), kind=kOutput, calls=%fused_computation.2 | convolution fusion | flops 182452224 | bytes 4751360 | tf_op jit(solution)/shard_map/sij,skj->ski/dot_general | solution.py:43
  203.6 20.4 %reduce-scatter.5.cloned.1.call-done = f32[2,16,128]{2,1,0:T(8,128)} async-done(((f32[8,16,128]{2,1,0:T(8,128)}), f32[2,16,128]{2,1,0:T(8,128)}) %reduce-scatter.5.cloned.1.call-update) | async-done | bytes 16400 | tf_op jit(solution)/shard_map/reduce_scatter | solution.py:52
  223.9 1.0 convolution_bitcast_fusion
  224.9 39.5 %psum.23 = f32[48,48]{0,1:T(8,128)S(1)} all-reduce(f32[48,48]{0,1:T(8,128)S(1)} %convolution_bitcast_fusion), channel_id=1, replica_groups=mesh['row'=8,'col'=4] {'row','col'}, use_global_device_ids=true, to_apply=%region_6.9 | all-reduce | flops 2304 | bytes 18432 | tf_op jit(solution)/shard_map/psum | solution.py:65
  265.3 0.9 fusion.26
  266.9 0.9 fusion.5
  267.8 0.8 fusion.4
  268.8 0.9 convolution_subtract_fusion.1
  269.7 0.9 convolution_subtract_fusion
  272.3 0.9 convolution_add_fusion
  273.2 1.5 cholesky.81
  276.0 1.2 custom-call.9
  (68 shorter events, 16.6 us)
Async XLA Ops:
  7.2 1.4 copy-start
  7.2 87.3 %copy-start.1 = (s32[1,1,58]{2,1,0:T(1,128)S(1)}, s32[1,1,58]{2,1,0:T(1,128)}, u32[]{:S(2)}) copy-start(s32[1,1,58]{2,1,0:T(1,128)} %param.10) | copy-start | bytes 700
  7.2 107.7 %reduce-scatter.3.cloned.1.call-start = ((), (), s32[]{:S(2)}) async-start(), calls=%async_computation.2 | async-start | bytes 81920 | tf_op jit(solution)/shard_map/reduce_scatter | solution.py:52
  95.5 128.4 %reduce-scatter.5.cloned.1.call-start = ((), (), s32[]{:S(2)}) async-start(), calls=%async_computation.3 | async-start | bytes 81920 | tf_op jit(solution)/shard_map/reduce_scatter | solution.py:52
Sparse Core Ops, SparseCore 0:
  95.6 19.2 reduce-scatter.2
  203.6 20.2 reduce-scatter.4
where the time goes:
time: 287 us; the launch traced here: 286 us
  blocking collectives  182 us (63%)
  waiting for transfers between devices  39.7 us (14%)
  matrix products  31.8 us (11%)
  between operations  14.8 us (5%)
  other arithmetic  12.8 us (4%)
  local copies, waits for them, and re-layouts  4.25 us (1%)
    psum x2, blocking collectives, on_device(): lax.psum(local_gram(stacked, stacked), ('row', 'col')) / row_total  79 us
    all_gather x2, blocking collectives, on_device(): gathered = lax.all_gather(vectors, 'row', axis=0, tiled=True)  61.3 us
    psum x1, blocking collectives, on_device(): lax.psum(local_gram(start_block, start_block), ('row', 'col')) / row_total  42 us
    reduce_scatter x2, waiting for transfers between devices, on_device(): lax.psum_scatter(jnp.einsum('rs,ski->rki', selector, operate_product, pre...  39.7 us
    dot_general x2, matrix products, on_device(): jnp.einsum('sij,skj->ski', matrix_tiles, gathered[cols_local], precision=...  16.1 us
    dot_general x22, matrix products, matmul(): jnp.dot(left, right, precision=highest, preferred_element_type=jnp.float32)  8.28 us
  transfers between devices with their start and end apart: 2, of which 2 were waited for; matrix products, arithmetic and copies ran while one was open for 0% of the time, Pallas kernels for 0%

commit v1 on v0

--- a/solution.py
+++ b/solution.py
@@ -62,7 +62,10 @@
             tiled=True,
         )
         stacked = jnp.concatenate([image_block, vectors, previous], axis=1)
-        all_means = lax.psum(local_gram(stacked, stacked), ("row", "col")) / row_total
+        all_means = (
+            jnp.sum(lax.all_gather(local_gram(stacked, stacked), ("row", "col")), axis=0)
+            / row_total
+        )
         yy_mean = all_means[:vec_count, :vec_count]
         vy_mean = all_means[vec_count : 2 * vec_count, :vec_count]
         py_mean = all_means[2 * vec_count :, :vec_count]

time: 287 us -> 289 us (level)
  blocking collectives: 182 us -> 189 us
  waiting for transfers between devices: 39.7 us -> 35.4 us
    all_gather x0 -> x2, blocking collectives: none -> 85.4 us  [on_device(): lax.all_gather(local_gram(stacked, stacked), ('row', 'col'))]
    psum x2 -> x0, blocking collectives: 79 us -> none  [on_device(): lax.psum(local_gram(stacked, stacked), ('row', 'col')) / row_total]
    reduce_scatter x2, waiting for transfers between devices: 39.7 us -> 35.4 us  [on_device(): lax.psum_scatter(jnp.einsum('rs,ski->rki', selector, operate_product, pre...]
where the time goes in v1:
time: 289 us; the launch traced here: 288 us
  blocking collectives  189 us (65%)
  waiting for transfers between devices  35.4 us (12%)
  matrix products  31.8 us (11%)
  between operations  14.8 us (5%)
  other arithmetic  12.9 us (4%)
  local copies, waits for them, and re-layouts  4.32 us (1%)
    all_gather x2, blocking collectives, on_device(): lax.all_gather(local_gram(stacked, stacked), ('row', 'col'))  85.4 us
    all_gather x2, blocking collectives, on_device(): gathered = lax.all_gather(vectors, 'row', axis=0, tiled=True)  61.3 us
    psum x1, blocking collectives, on_device(): lax.psum(local_gram(start_block, start_block), ('row', 'col')) / row_total  42 us
    reduce_scatter x2, waiting for transfers between devices, on_device(): lax.psum_scatter(jnp.einsum('rs,ski->rki', selector, operate_product, pre...  35.4 us
    dot_general x2, matrix products, on_device(): jnp.einsum('sij,skj->ski', matrix_tiles, gathered[cols_local], precision=...  16.1 us
    dot_general x22, matrix products, matmul(): jnp.dot(left, right, precision=highest, preferred_element_type=jnp.float32)  8.29 us
  transfers between devices with their start and end apart: 2, of which 2 were waited for; matrix products, arithmetic and copies ran while one was open for 0% of the time, Pallas kernels for 0%

profile of v1, /device:TPU:0, one launch (start us, length us, event | category | flops | bytes accessed | tf_op | source)
XLA Modules:
  0.0 288.0 jit_solution(13248571649721391608)
XLA Ops:
  8.7 42.0 %psum.7 = f32[16,16]{0,1:T(8,128)S(1)} all-reduce(f32[16,16]{0,1:T(8,128)S(1)} %convolution_bitcast_fusion.12), channel_id=1, replica_groups=mesh['row'=8,'col'=4] {'row','col'}, use_global_device_ids=true, to_apply=%region_0.0 | all-reduce | flops 256 | bytes 2048 | tf_op jit(solution)/shard_map/psum | solution.py:31
  50.8 1.5 cholesky.59
  53.6 1.2 custom-call.7
  55.1 30.6 %all_gather.18 = f32[16,16,128]{2,1,0:T(8,128)S(1)} all-gather(f32[2,16,128]{2,1,0:T(8,128)S(1)} %convolution_bitcast_fusion.8), channel_id=1, replica_groups=mesh['row'=8,'col'=4] {'row'}, dimensions={0}, use_global_device_ids=true | all-gather | bytes 147456 | tf_op jit(solution)/shard_map/all_gather | solution.py:42
  86.4 8.1 %fusion.2 = f32[58,16,128]{2,1,0:T(8,128)S(1)} fusion(f32[58,16,128]{2,1,0:T(8,128)S(1)} %gather_fusion, f32[1,1,58,128,128]{4,3,2,1,0:T(8,128)} %param.9), kind=kOutput, calls=%fused_computation.4 | convolution fusion | flops 182452224 | bytes 4751360 | tf_op jit(solution)/shard_map/sij,skj->ski/dot_general | solution.py:43
  95.5 19.3 %reduce-scatter.3.cloned.1.call-done = f32[2,16,128]{2,1,0:T(8,128)} async-done(((f32[8,16,128]{2,1,0:T(8,128)}), f32[2,16,128]{2,1,0:T(8,128)}) %reduce-scatter.3.cloned.1.call-update) | async-done | bytes 16400 | tf_op jit(solution)/shard_map/reduce_scatter | solution.py:52
  114.9 1.0 convolution_bitcast_fusion.1
  115.8 42.7 %all-gather = f32[1536,48]{1,0:T(8,128)S(1)} all-gather(f32[48,48]{1,0:T(8,128)S(1)} %convolution_bitcast_fusion.1), channel_id=2, replica_groups=mesh['row'=8,'col'=4] {'row','col'}, dimensions={0}, use_global_device_ids=true | all-gather | bytes 304128 | tf_op jit(solution)/shard_map/all_gather | solution.py:66
  159.7 0.9 fusion.7
  162.0 1.5 cholesky.70
  164.8 1.2 custom-call.8
  166.3 30.7 %all_gather.21 = f32[16,16,128]{2,1,0:T(8,128)S(1)} all-gather(f32[2,16,128]{2,1,0:T(8,128)S(1)} %convolution_bitcast_fusion.5), channel_id=1, replica_groups=mesh['row'=8,'col'=4] {'row'}, dimensions={0}, use_global_device_ids=true | all-gather | bytes 147456 | tf_op jit(solution)/shard_map/all_gather | solution.py:42
  197.7 8.1 %fusion = f32[58,16,128]{2,1,0:T(8,128)S(1)} fusion(f32[58,16,128]{2,1,0:T(8,128)S(1)} %gather_fusion.1, f32[1,1,58,128,128]{4,3,2,1,0:T(8,128)} %param.9), kind=kOutput, calls=%fused_computation.2 | convolution fusion | flops 182452224 | bytes 4751360 | tf_op jit(solution)/shard_map/sij,skj->ski/dot_general | solution.py:43
  206.8 16.0 %reduce-scatter.5.cloned.1.call-done = f32[2,16,128]{2,1,0:T(8,128)} async-done(((f32[8,16,128]{2,1,0:T(8,128)}), f32[2,16,128]{2,1,0:T(8,128)}) %reduce-scatter.5.cloned.1.call-update) | async-done | bytes 16400 | tf_op jit(solution)/shard_map/reduce_scatter | solution.py:52
  222.8 1.0 convolution_bitcast_fusion
  223.8 42.7 %all-gather.1 = f32[1536,48]{1,0:T(8,128)S(1)} all-gather(f32[48,48]{1,0:T(8,128)S(1)} %convolution_bitcast_fusion), channel_id=3, replica_groups=mesh['row'=8,'col'=4] {'row','col'}, dimensions={0}, use_global_device_ids=true | all-gather | bytes 304128 | tf_op jit(solution)/shard_map/all_gather | solution.py:66
  267.6 0.9 fusion.26
  269.1 0.9 fusion.5
  271.8 0.9 convolution_subtract_fusion.1
  272.6 0.9 convolution_subtract_fusion
  273.5 0.9 convolution_add_fusion.2
  274.5 0.9 convolution_add_fusion
  275.5 1.5 cholesky.81
  278.2 1.2 custom-call.9
  (71 shorter events, 16.8 us)
Async XLA Ops:
  7.2 1.4 copy-start
  7.2 87.3 %copy-start.1 = (s32[1,1,58]{2,1,0:T(1,128)S(1)}, s32[1,1,58]{2,1,0:T(1,128)}, u32[]{:S(2)}) copy-start(s32[1,1,58]{2,1,0:T(1,128)} %param.10) | copy-start | bytes 700
  7.2 107.7 %reduce-scatter.3.cloned.1.call-start = ((), (), s32[]{:S(2)}) async-start(), calls=%async_computation.2 | async-start | bytes 81920 | tf_op jit(solution)/shard_map/reduce_scatter | solution.py:52
  95.5 127.4 %reduce-scatter.5.cloned.1.call-start = ((), (), s32[]{:S(2)}) async-start(), calls=%async_computation.3 | async-start | bytes 81920 | tf_op jit(solution)/shard_map/reduce_scatter | solution.py:52
Sparse Core Ops, SparseCore 0:
  95.6 19.2 reduce-scatter.2
  206.9 15.8 reduce-scatter.4
